TPU v7x, 32 devices: a whole 2x2x4 slice. The times are simulated.
32 devices in a mesh: section: 2 (over y), design: 8 (over z, x), batch: 2 (over core).
Axes of the slice: x: 2, y: 2, z: 4, core: 2. Of those that a mesh axis runs over, the one named last changes fastest.
Arguments:
- samples: float32 [64, 4096], replicated, may hold values from -6 to 6
- order: int32 [4096], P('batch'), may hold values from 0 to 4095, each once
- design_points: bfloat16 [2, 64, 16384], P('section', None, 'design'), may hold values from -6 to 6
- weights: bfloat16 [2, 64, 16384], P('section', None, 'design'), may hold values from -2 to 2
- length_sq: float32 [2, 64], replicated, may hold values from 8 to 128
Outputs:
- moments: float32 [2, 4, 64, 1024], P('section', None, None, ('batch', 'design'))
Inputs may be any that keep to these rules, and one draw needn't show every extreme that they name: `order`: each sample index appears exactly once.
All inputs are finite; a program needn't handle non-finite values.
Results may differ from a plain program's by a relative error of at most 0.0037.
Values may be sent and summed in bfloat16 or wider, within the bound.
A program may use at most 64 MiB of HBM per device.

v0:
```python
import jax
import jax.numpy as jnp
from jax import lax
from jax.sharding import PartitionSpec as P

MICRO = 512


def passed_along(block, axis, distance):
    devices = range(lax.axis_size(axis))
    route = [(i - distance, i) for i in devices if i - distance in devices]
    return lax.ppermute(block, axis, route)


def local_sum(mean_in, var_in, points, squares, weight_rows, lengths):
    denom = lengths[:, None] + 2.0 * var_in
    offset = jnp.sum(mean_in * mean_in / denom, axis=0)
    log_scale = -0.5 * jnp.sum(jnp.log(1.0 + 2.0 * var_in / lengths[:, None]), axis=0)
    scaled = (mean_in / denom).astype(jnp.bfloat16)
    inverse = (1.0 / denom).astype(jnp.bfloat16)
    cross = lax.dot_general(
        scaled, points, (((0,), (0,)), ((), ())), preferred_element_type=jnp.float32
    )
    quad = lax.dot_general(
        inverse, squares, (((0,), (0,)), ((), ())), preferred_element_type=jnp.float32
    )
    kernel = jnp.exp(log_scale[:, None] - offset[:, None] + 2.0 * cross - quad).astype(jnp.bfloat16)
    return lax.dot_general(
        weight_rows, kernel, (((1,), (1,)), ((), ())), preferred_element_type=jnp.float32
    )


def square_of(points):
    wide = points.astype(jnp.float32)
    return (wide * wide).astype(jnp.bfloat16)


def shards(samples, order, design_points, weights, length_sq):
    section_index = lax.axis_index("section")
    is_first = section_index == 0
    points = design_points[0]
    weight_rows = weights[0]
    lengths = jnp.where(is_first, length_sq[0], length_sq[1])
    squares = square_of(points)
    feat = points.shape[0]
    half = feat // 2
    count = order.shape[0] // MICRO
    share = MICRO // lax.axis_size("design")
    column = lax.axis_index("design") * share

    def pick(turn):
        indices = order[turn * MICRO : (turn + 1) * MICRO]
        return jnp.take(samples, indices, axis=1)

    received = jnp.zeros((feat, MICRO), jnp.float32)
    zeros_rest = jnp.zeros((feat - half, MICRO), jnp.float32)
    firsts = []
    seconds = []
    for turn in range(count + 1):
        current = pick(min(turn, count - 1))
        earlier = pick(max(turn - 1, 0))
        moments_in = received
        later_mean = jnp.concatenate([moments_in[:half], earlier[half:]], axis=0)
        later_var = jnp.concatenate([moments_in[half:], zeros_rest], axis=0)
        mean_in = jnp.where(is_first, current, later_mean)
        var_in = jnp.where(is_first, 0.0, later_var)
        partial_sum = local_sum(mean_in, var_in, points, squares, weight_rows, lengths)
        summed = lax.psum(partial_sum, "design")
        layer_out = jnp.where(
            is_first,
            jnp.concatenate([summed[:half], jax.nn.softplus(summed[half:])], axis=0),
            summed,
        )
        received = passed_along(layer_out, "section", 1)
        block = lax.dynamic_slice_in_dim(layer_out, column, share, 1)
        if turn < count:
            firsts.append(block)
        if turn > 0:
            seconds.append(block)
    result = jnp.where(is_first, jnp.stack(firsts, axis=0), jnp.stack(seconds, axis=0))
    return result[None]


def solution(mesh):
    placed = (P(), P("batch"), P("section", None, "design"), P("section", None, "design"), P())
    return jax.shard_map(
        shards,
        mesh=mesh,
        in_specs=placed,
        out_specs=P("section", None, None, ("batch", "design")),
        check_vma=False,
    )
```

profile of v0, /device:TPU:0, one launch (start us, length us, event | category | flops | bytes accessed | tf_op | source)
XLA Modules:
  0.0 447.8 jit_solution(6106497824247773900)
XLA Ops:
  6.5 0.0 copy-start
  6.5 0.8 compare_and_fusion
  7.3 0.8 compare_select_fusion.5
  8.1 0.8 divide_convert_fusion.22
  8.9 0.6 log_reduce_fusion.4
  9.5 1.8 copy.6
  11.3 1.0 gather_fusion
  12.4 0.1 copy.7
  12.5 0.1 fusion.29
  12.6 2.7 fusion.23
  16.1 4.4 fusion.9
  20.5 0.0 all-reduce.11.cloned.1.call-update
  20.5 0.0 all-reduce.13.cloned.1.call-start
  20.5 73.3 %all-reduce.11.cloned.1.call-done = f32[64,512]{1,0:T(8,128)} async-done(((f32[64,512]{1,0:T(8,128)}), f32[64,512]{1,0:T(8,128)}) %all-reduce.11.cloned.1.call-update) | async-done | bytes 131088 | tf_op jit(solution)/shard_map/psum | solution.py:68
  93.8 0.9 fusion.144
  94.8 4.3 collective-permute-start
  99.1 1.0 gather_fusion.1
  100.1 0.1 copy.9
  100.3 1.3 collective-permute-done
  101.6 0.1 log_reduce_fusion.3
  101.7 2.7 fusion.21
  104.5 4.4 fusion.8
  108.9 0.0 all-reduce.13.cloned.1.call-update
  108.9 0.0 all-reduce.15.cloned.1.call-start
  109.0 70.6 %all-reduce.13.cloned.1.call-done = f32[64,512]{1,0:T(8,128)} async-done(((f32[64,512]{1,0:T(8,128)}), f32[64,512]{1,0:T(8,128)}) %all-reduce.13.cloned.1.call-update) | async-done | bytes 131088 | tf_op jit(solution)/shard_map/psum | solution.py:68
  179.6 0.9 fusion.142
  180.6 4.9 %collective-permute-start.1 = (f32[64,512]{1,0:T(8,128)S(1)}, f32[64,512]{1,0:T(8,128)}, u32[]{:S(2)}, u32[]{:S(2)}) collective-permute-start(f32[64,512]{1,0:T(8,128)S(1)} %maximum_select_fusion.2), channel_id=1, source_target_pairs={{0,16},{1,17},{2,18},{3,19},{4,20},{5,21},{6,22},{7,23},{8,24},{9,... | collective-permute-start | bytes 393224 | tf_op jit(solution)/shard_map/ppermute | solution.py:12
  185.5 1.0 gather_fusion.2
  186.5 0.1 copy.11
  186.7 0.7 collective-permute-done.1
  187.3 0.9 fusion.141
  188.2 0.1 log_reduce_fusion.2
  188.4 2.7 fusion.19
  191.1 4.4 fusion.7
  195.5 0.0 all-reduce.15.cloned.1.call-update
  195.5 0.0 all-reduce.17.cloned.1.call-start
  195.6 70.7 %all-reduce.15.cloned.1.call-done = f32[64,512]{1,0:T(8,128)} async-done(((f32[64,512]{1,0:T(8,128)}), f32[64,512]{1,0:T(8,128)}) %all-reduce.15.cloned.1.call-update) | async-done | bytes 131088 | tf_op jit(solution)/shard_map/psum | solution.py:68
  266.3 0.9 fusion.140
  267.3 4.9 %collective-permute-start.2 = (f32[64,512]{1,0:T(8,128)S(1)}, f32[64,512]{1,0:T(8,128)}, u32[]{:S(2)}, u32[]{:S(2)}) collective-permute-start(f32[64,512]{1,0:T(8,128)S(1)} %maximum_select_fusion.4), channel_id=1, source_target_pairs={{0,16},{1,17},{2,18},{3,19},{4,20},{5,21},{6,22},{7,23},{8,24},{9,... | collective-permute-start | bytes 393224 | tf_op jit(solution)/shard_map/ppermute | solution.py:12
  272.2 1.0 gather_fusion.3
  273.2 0.1 copy.13
  273.4 0.7 collective-permute-done.2
  274.1 0.9 fusion.139
  275.0 0.1 log_reduce_fusion.1
  275.1 2.7 fusion.17
  277.8 4.4 fusion.6
  282.2 0.0 all-reduce.17.cloned.1.call-update
  282.3 0.0 all-reduce.19.cloned.1.call-start
  282.3 70.8 %all-reduce.17.cloned.1.call-done = f32[64,512]{1,0:T(8,128)} async-done(((f32[64,512]{1,0:T(8,128)}), f32[64,512]{1,0:T(8,128)}) %all-reduce.17.cloned.1.call-update) | async-done | bytes 131088 | tf_op jit(solution)/shard_map/psum | solution.py:68
  353.1 0.9 fusion.138
  354.0 4.3 collective-permute-start.3
  358.3 0.1 dynamic-slice_bitcast_fusion.3
  358.4 0.1 dynamic-slice_bitcast_fusion.2
  358.5 2.3 collective-permute-done.3
  360.8 0.1 log_reduce_fusion
  361.0 2.7 fusion.15
  363.7 4.4 fusion.5
  368.1 0.0 all-reduce.19.cloned.1.call-update
  368.1 0.1 dynamic-slice_bitcast_fusion.1
  368.2 0.1 dynamic-slice_bitcast_fusion
  368.3 70.5 %all-reduce.19.cloned.1.call-done = f32[64,512]{1,0:T(8,128)} async-done(((f32[64,512]{1,0:T(8,128)}), f32[64,512]{1,0:T(8,128)}) %all-reduce.19.cloned.1.call-update) | async-done | bytes 131088 | tf_op jit(solution)/shard_map/psum | solution.py:68
  438.8 0.9 compare_select_fusion
  439.8 0.8 fusion.94
  440.6 0.7 maximum_select_fusion.7
  (22 shorter events, 0.2 us)
Async XLA Ops:
  6.5 9.5 %copy-start = (bf16[1,64,2048]{2,1,0:T(8,128)(2,1)S(1)}, bf16[1,64,2048]{2,1,0:T(8,128)(2,1)}, u32[]{:S(2)}) copy-start(bf16[1,64,2048]{2,1,0:T(8,128)(2,1)} %param.10) | copy-start | bytes 786436
  6.5 6.1 %copy-start.1 = (bf16[1,64,2048]{2,1,0:T(8,128)(2,1)S(1)}, bf16[1,64,2048]{2,1,0:T(8,128)(2,1)}, u32[]{:S(2)}) copy-start(bf16[1,64,2048]{2,1,0:T(8,128)(2,1)} %param.9) | copy-start | bytes 786436
  6.5 87.3 %all-reduce.11.cloned.1.call-start = ((), (), s32[]{:S(2)}) async-start(), calls=%async_computation | async-start | bytes 262144 | tf_op jit(solution)/shard_map/psum | solution.py:68
  20.5 159.1 %all-reduce.13.cloned.1.call-start = ((), (), s32[]{:S(2)}) async-start(), calls=%async_computation.1 | async-start | bytes 262144 | tf_op jit(solution)/shard_map/psum | solution.py:68
  94.8 6.8 %collective-permute-start = (f32[64,512]{1,0:T(8,128)S(1)}, f32[64,512]{1,0:T(8,128)S(1)}, u32[]{:S(2)}, u32[]{:S(2)}) collective-permute-start(f32[64,512]{1,0:T(8,128)S(1)} %maximum_select_fusion), channel_id=1, source_target_pairs={{0,16},{1,17},{2,18},{3,19},{4,20},{5,21},{6,22},{7,23},{8,24},{9,... | collective-permute-start | bytes 393224 | tf_op jit(solution)/shard_map/ppermute | solution.py:12
  108.9 157.4 %all-reduce.15.cloned.1.call-start = ((), (), s32[]{:S(2)}) async-start(), calls=%async_computation.2 | async-start | bytes 262144 | tf_op jit(solution)/shard_map/psum | solution.py:68
  180.6 6.8 %collective-permute-start.1 = (f32[64,512]{1,0:T(8,128)S(1)}, f32[64,512]{1,0:T(8,128)}, u32[]{:S(2)}, u32[]{:S(2)}) collective-permute-start(f32[64,512]{1,0:T(8,128)S(1)} %maximum_select_fusion.2), channel_id=1, source_target_pairs={{0,16},{1,17},{2,18},{3,19},{4,20},{5,21},{6,22},{7,23},{8,24},{9,... | collective-permute-start | bytes 393224 | tf_op jit(solution)/shard_map/ppermute | solution.py:12
  195.5 157.5 %all-reduce.17.cloned.1.call-start = ((), (), s32[]{:S(2)}) async-start(), calls=%async_computation.3 | async-start | bytes 262144 | tf_op jit(solution)/shard_map/psum | solution.py:68
  267.3 6.8 %collective-permute-start.2 = (f32[64,512]{1,0:T(8,128)S(1)}, f32[64,512]{1,0:T(8,128)}, u32[]{:S(2)}, u32[]{:S(2)}) collective-permute-start(f32[64,512]{1,0:T(8,128)S(1)} %maximum_select_fusion.4), channel_id=1, source_target_pairs={{0,16},{1,17},{2,18},{3,19},{4,20},{5,21},{6,22},{7,23},{8,24},{9,... | collective-permute-start | bytes 393224 | tf_op jit(solution)/shard_map/ppermute | solution.py:12
  282.3 156.6 %all-reduce.19.cloned.1.call-start = ((), (), s32[]{:S(2)}) async-start(), calls=%async_computation.4 | async-start | bytes 262144 | tf_op jit(solution)/shard_map/psum | solution.py:68
  354.0 6.8 %collective-permute-start.3 = (f32[64,512]{1,0:T(8,128)S(1)}, f32[64,512]{1,0:T(8,128)S(1)}, u32[]{:S(2)}, u32[]{:S(2)}) collective-permute-start(f32[64,512]{1,0:T(8,128)S(1)} %maximum_select_fusion.6), channel_id=1, source_target_pairs={{0,16},{1,17},{2,18},{3,19},{4,20},{5,21},{6,22},{7,23},{8,24},{9,... | collective-permute-start | bytes 393224 | tf_op jit(solution)/shard_map/ppermute | solution.py:12
Sparse Core Ops, SparseCore 0:
  20.6 73.1 all-reduce.10
  109.0 70.5 all-reduce.12
  195.7 70.6 all-reduce.14
  282.4 70.6 all-reduce.16
  368.3 70.5 all-reduce.18
where the time goes:
time: 449 us; the launch traced here: 448 us
  waiting for transfers between devices  361 us (80%)
  matrix products  35.7 us (8%)
  starting transfers between devices  18.6 us (4%)
  between operations  14 us (3%)
  other arithmetic  9.83 us (2%)
  local copies, waits for them, and re-layouts  8.53 us (2%)
    psum x5, waiting for transfers between devices, shards(): summed = lax.psum(partial_sum, 'design')  356 us
    dot_general x5, matrix products, local_sum(): lax.dot_general(weight_rows, kernel, (((1,), (1,)), ((), ())), preferred_...  22.1 us
    ppermute x4, starting transfers between devices, passed_along(): return lax.ppermute(block, axis, route)  18.4 us
    dot_general x5, matrix products, local_sum(): lax.dot_general(scaled, points, (((0,), (0,)), ((), ())), preferred_eleme...  13.6 us
  transfers between devices with their start and end apart: 9, of which 9 were waited for; matrix products, arithmetic and copies ran while one was open for 1% of the time, Pallas kernels for 0%

commit v1 on v0

--- a/solution.py
+++ b/solution.py
@@ -65,7 +65,7 @@
         mean_in = jnp.where(is_first, current, later_mean)
         var_in = jnp.where(is_first, 0.0, later_var)
         partial_sum = local_sum(mean_in, var_in, points, squares, weight_rows, lengths)
-        summed = lax.psum(partial_sum, "design")
+        summed = lax.all_gather(partial_sum, "design").sum(axis=0)
         layer_out = jnp.where(
             is_first,
             jnp.concatenate([summed[:half], jax.nn.softplus(summed[half:])], axis=0),

time: 449 us -> 305 us (0.68)
  waiting for transfers between devices: 361 us -> 211 us
  other arithmetic: 9.83 us -> 16.4 us
    psum x5 -> x0, waiting for transfers between devices: 356 us -> none  [shards(): summed = lax.psum(partial_sum, 'design')]
    all_gather x0 -> x5, waiting for transfers between devices: none -> 201 us  [shards(): summed = lax.all_gather(partial_sum, 'design').sum(axis=0)]
    reduce_sum x0 -> x5, other arithmetic: none -> 6.53 us  [shards(): summed = lax.all_gather(partial_sum, 'design').sum(axis=0)]
    ppermute x4, waiting for transfers between devices: 5.04 us -> 10.1 us  [passed_along(): return lax.ppermute(block, axis, route)]
  transfers between devices with their start and end apart: 9 -> 9, of which waited for: 9 -> 9; matrix products, arithmetic and copies ran while one was open for 1% -> 2% of each run, Pallas kernels for 0% -> 0%
where the time goes in v1:
time: 305 us; the launch traced here: 304 us
  waiting for transfers between devices  211 us (69%)
  matrix products  35.2 us (12%)
  other arithmetic  16.4 us (5%)
  starting transfers between devices  14.6 us (5%)
  between operations  14.1 us (5%)
  local copies, waits for them, and re-layouts  12.8 us (4%)
    all_gather x5, waiting for transfers between devices, shards(): summed = lax.all_gather(partial_sum, 'design').sum(axis=0)  201 us
    dot_general x5, matrix products, local_sum(): lax.dot_general(weight_rows, kernel, (((1,), (1,)), ((), ())), preferred_...  21.7 us
    ppermute x4, starting transfers between devices, passed_along(): return lax.ppermute(block, axis, route)  14.4 us
    dot_general x5, matrix products, local_sum(): lax.dot_general(scaled, points, (((0,), (0,)), ((), ())), preferred_eleme...  13.5 us
    ppermute x4, waiting for transfers between devices, passed_along(): return lax.ppermute(block, axis, route)  10.1 us
    reduce_sum x5, other arithmetic, shards(): summed = lax.all_gather(partial_sum, 'design').sum(axis=0)  6.53 us
  transfers between devices with their start and end apart: 9, of which 9 were waited for; matrix products, arithmetic and copies ran while one was open for 2% of the time, Pallas kernels for 0%

profile of v1, /device:TPU:0, one launch (start us, length us, event | category | flops | bytes accessed | tf_op | source)
XLA Modules:
  0.0 304.3 jit_solution(6445253951246476393)
XLA Ops:
  6.5 0.8 compare_and_fusion
  7.3 0.8 compare_select_fusion.5
  8.1 0.8 divide_convert_fusion.22
  8.9 0.6 log_reduce_fusion.4
  9.5 1.8 copy.19
  11.3 1.0 gather_fusion
  12.4 0.1 select_bitcast_fusion.3
  12.5 0.1 slice.127
  12.7 0.3 fusion.25
  13.0 2.7 fusion.23
  16.3 4.4 %fusion.5 = f32[64,512]{1,0:T(8,128)} fusion(f32[512,2048]{1,0:T(8,128)} %fusion.23, f32[512]{0:T(512)S(1)} %broadcast_subtract_fusion, bf16[1,64,2048]{2,1,0:T(8,128)(2,1)S(1)} %copy-done, bf16[1,64,2048]{2,1,0:T(8,128)(2,1)S(1)} %copy-done.1, bf16[64]{0:T(256)(128)(2,1)S(1)} %get-tuple-element.17), kind=kOutput, calls=%fused_computation.14 | convolution fusion | flops 273022976 | bytes 4851840 | tf_op jit(solution)/shard_map/dot_general | solution.py:28
  20.8 43.1 %all-gather.11.cloned.1.call-done = f32[512,512]{1,0:T(8,128)} async-done(((f32[64,512]{1,0:T(8,128)}), f32[512,512]{1,0:T(8,128)}) %all-gather.11.cloned.1.call-update) | async-done | bytes 1048592 | tf_op jit(solution)/shard_map/all_gather | solution.py:68
  63.9 1.3 reduce_sum.137
  65.4 0.2 fusion.98
  65.6 0.1 maximum_select_fusion
  65.7 3.4 %collective-permute-start = (f32[64,512]{0,1:T(8,128)S(1)}, f32[64,512]{0,1:T(8,128)S(1)}, u32[]{:S(2)}, u32[]{:S(2)}) collective-permute-start(f32[64,512]{0,1:T(8,128)S(1)} %maximum_select_fusion), channel_id=1, source_target_pairs={{0,16},{1,17},{2,18},{3,19},{4,20},{5,21},{6,22},{7,23},{8,24},{9,... | collective-permute-start | bytes 393224 | tf_op jit(solution)/shard_map/ppermute | solution.py:12
  69.2 1.6 gather_fusion.1
  70.8 2.2 collective-permute-done
  73.0 0.1 fusion.97
  73.1 1.3 log_reduce_fusion.3
  74.5 2.7 fusion.21
  77.2 4.3 %fusion.9 = f32[64,512]{1,0:T(8,128)} fusion(f32[512,2048]{1,0:T(8,128)} %fusion.21, f32[512]{0:T(512)S(1)} %multiply_subtract_fusion.3, bf16[1,64,2048]{2,1,0:T(8,128)(2,1)S(1)} %copy-done, bf16[1,64,2048]{2,1,0:T(8,128)(2,1)S(1)} %copy-done.1, f32[64]{0:T(128)S(1)} %get-tuple-element.18, f32[32,512]{0,1:T(8,128)S(1)} %get-tuple-element.32, pred[]{:T(512)S(6)} %eq.3), kind=kOutput, calls=%fused_computation.18 | convolution fusion | flops 273186816 | bytes 4917505 | tf_op jit(solution)/shard_map/dot_general | solution.py:28
  81.6 40.1 %all-gather.13.cloned.1.call-done = f32[512,512]{1,0:T(8,128)} async-done(((f32[64,512]{1,0:T(8,128)}), f32[512,512]{1,0:T(8,128)}) %all-gather.13.cloned.1.call-update) | async-done | bytes 1048592 | tf_op jit(solution)/shard_map/all_gather | solution.py:68
  121.7 1.3 reduce_sum.140
  123.1 0.2 fusion.96
  123.3 0.1 maximum_select_fusion.2
  123.5 4.1 %collective-permute-start.1 = (f32[64,512]{0,1:T(8,128)S(1)}, f32[64,512]{0,1:T(8,128)}, u32[]{:S(2)}, u32[]{:S(2)}) collective-permute-start(f32[64,512]{0,1:T(8,128)S(1)} %maximum_select_fusion.2), channel_id=1, source_target_pairs={{0,16},{1,17},{2,18},{3,19},{4,20},{5,21},{6,22},{7,23},{8,24},{9,... | collective-permute-start | bytes 393224 | tf_op jit(solution)/shard_map/ppermute | solution.py:12
  127.6 1.6 gather_fusion.2
  129.4 1.4 collective-permute-done.1
  130.8 1.2 fusion.95
  131.9 1.3 log_reduce_fusion.2
  133.2 2.7 fusion.19
  135.9 4.3 %fusion.8 = f32[64,512]{1,0:T(8,128)} fusion(f32[512,2048]{1,0:T(8,128)} %fusion.19, f32[512]{0:T(512)S(1)} %multiply_subtract_fusion.2, bf16[1,64,2048]{2,1,0:T(8,128)(2,1)S(1)} %copy-done, bf16[1,64,2048]{2,1,0:T(8,128)(2,1)S(1)} %copy-done.1, f32[64]{0:T(128)S(1)} %get-tuple-element.18, f32[32,512]{0,1:T(8,128)S(1)} %get-tuple-element.28, pred[]{:T(512)S(6)} %eq.3), kind=kOutput, calls=%fused_computation.17 | convolution fusion | flops 273186816 | bytes 4917505 | tf_op jit(solution)/shard_map/dot_general | solution.py:28
  140.4 40.2 %all-gather.15.cloned.1.call-done = f32[512,512]{1,0:T(8,128)} async-done(((f32[64,512]{1,0:T(8,128)}), f32[512,512]{1,0:T(8,128)}) %all-gather.15.cloned.1.call-update) | async-done | bytes 1048592 | tf_op jit(solution)/shard_map/all_gather | solution.py:68
  180.6 1.3 reduce_sum.143
  182.0 0.2 fusion.94
  182.2 0.8 maximum_select_fusion.4
  183.1 3.6 %collective-permute-start.2 = (f32[64,512]{0,1:T(8,128)}, f32[64,512]{0,1:T(8,128)S(1)}, u32[]{:S(2)}, u32[]{:S(2)}) collective-permute-start(f32[64,512]{0,1:T(8,128)} %maximum_select_fusion.4), channel_id=1, source_target_pairs={{0,16},{1,17},{2,18},{3,19},{4,20},{5,21},{6,22},{7,23},{8,24},{9,... | collective-permute-start | bytes 393224 | tf_op jit(solution)/shard_map/ppermute | solution.py:12
  186.7 1.0 gather_fusion.3
  187.7 0.1 slice.141
  187.8 2.8 collective-permute-done.2
  190.6 0.1 fusion.93
  190.8 0.4 log_reduce_fusion.1
  191.2 2.7 fusion.17
  193.9 4.3 %fusion.7 = f32[64,512]{1,0:T(8,128)} fusion(f32[512,2048]{1,0:T(8,128)} %fusion.17, f32[512]{0:T(512)S(1)} %multiply_subtract_fusion.1, bf16[1,64,2048]{2,1,0:T(8,128)(2,1)S(1)} %copy-done, bf16[1,64,2048]{2,1,0:T(8,128)(2,1)S(1)} %copy-done.1, f32[64]{0:T(128)S(1)} %get-tuple-element.18, f32[32,512]{0,1:T(8,128)S(1)} %get-tuple-element.24, pred[]{:T(512)S(6)} %eq.3), kind=kOutput, calls=%fused_computation.16 | convolution fusion | flops 273186816 | bytes 4917505 | tf_op jit(solution)/shard_map/dot_general | solution.py:28
  198.3 40.0 %all-gather.17.cloned.1.call-done = f32[512,512]{1,0:T(8,128)} async-done(((f32[64,512]{1,0:T(8,128)}), f32[512,512]{1,0:T(8,128)}) %all-gather.17.cloned.1.call-update) | async-done | bytes 1048592 | tf_op jit(solution)/shard_map/all_gather | solution.py:68
  238.3 1.3 reduce_sum.146
  239.7 0.2 fusion.92
  239.9 0.1 maximum_select_fusion.6
  240.1 3.4 %collective-permute-start.3 = (f32[64,512]{0,1:T(8,128)S(1)}, f32[64,512]{0,1:T(8,128)S(1)}, u32[]{:S(2)}, u32[]{:S(2)}) collective-permute-start(f32[64,512]{0,1:T(8,128)S(1)} %maximum_select_fusion.6), channel_id=1, source_target_pairs={{0,16},{1,17},{2,18},{3,19},{4,20},{5,21},{6,22},{7,23},{8,24},{9,... | collective-permute-start | bytes 393224 | tf_op jit(solution)/shard_map/ppermute | solution.py:12
  243.5 0.1 slice.146
  243.6 3.7 %collective-permute-done.3 = f32[64,512]{0,1:T(8,128)S(1)} collective-permute-done((f32[64,512]{0,1:T(8,128)S(1)}, f32[64,512]{0,1:T(8,128)S(1)}, u32[]{:S(2)}, u32[]{:S(2)}) %collective-permute-start.3) | collective-permute-done | bytes 131104 | tf_op jit(solution)/shard_map/ppermute | solution.py:12
  247.3 0.1 fusion.91
  247.5 0.3 log_reduce_fusion
  247.8 2.7 fusion.15
  250.5 4.3 %fusion.6 = f32[64,512]{1,0:T(8,128)} fusion(f32[512,2048]{1,0:T(8,128)} %fusion.15, f32[512]{0:T(512)S(1)} %multiply_subtract_fusion, bf16[1,64,2048]{2,1,0:T(8,128)(2,1)S(1)} %copy-done, bf16[1,64,2048]{2,1,0:T(8,128)(2,1)S(1)} %copy-done.1, f32[64]{0:T(128)S(1)} %get-tuple-element.18, f32[32,512]{0,1:T(8,128)S(1)} %get-tuple-element.20, pred[]{:T(512)S(6)} %eq.3), kind=kOutput, calls=%fused_computation.15 | convolution fusion | flops 273186816 | bytes 4917505 | tf_op jit(solution)/shard_map/dot_general | solution.py:28
  254.9 0.8 constant_dynamic-slice_fusion.4
  255.7 0.8 constant_dynamic-slice_fusion.3
  256.5 0.8 constant_dynamic-slice_fusion.2
  257.5 37.5 %all-gather.19.cloned.1.call-done = f32[512,512]{1,0:T(8,128)} async-done(((f32[64,512]{1,0:T(8,128)}), f32[512,512]{1,0:T(8,128)}) %all-gather.19.cloned.1.call-update) | async-done | bytes 1048592 | tf_op jit(solution)/shard_map/all_gather | solution.py:68
  295.0 1.3 reduce_sum.149
  296.5 0.1 copy.44
  296.6 0.1 compare_select_fusion
  297.1 0.7 maximum_select_fusion.8
  (43 shorter events, 1.7 us)
Async XLA Ops:
  6.5 9.8 %copy-start = (bf16[1,64,2048]{2,1,0:T(8,128)(2,1)S(1)}, bf16[1,64,2048]{2,1,0:T(8,128)(2,1)}, u32[]{:S(2)}) copy-start(bf16[1,64,2048]{2,1,0:T(8,128)(2,1)} %param.10) | copy-start | bytes 786436
  6.5 6.4 %copy-start.1 = (bf16[1,64,2048]{2,1,0:T(8,128)(2,1)S(1)}, bf16[1,64,2048]{2,1,0:T(8,128)(2,1)}, u32[]{:S(2)}) copy-start(bf16[1,64,2048]{2,1,0:T(8,128)(2,1)} %param.9) | copy-start | bytes 786436
  6.5 57.4 %all-gather.11.cloned.1.call-start = ((), (), s32[]{:S(2)}) async-start(), calls=%async_computation | async-start | bytes 1179648 | tf_op jit(solution)/shard_map/all_gather | solution.py:68
  20.8 100.9 %all-gather.13.cloned.1.call-start = ((), (), s32[]{:S(2)}) async-start(), calls=%async_computation.1 | async-start | bytes 1179648 | tf_op jit(solution)/shard_map/all_gather | solution.py:68
  65.7 5.1 %copy-start.2 = (f32[64,512]{0,1:T(8,128)}, f32[64,512]{0,1:T(8,128)S(1)}, u32[]{:S(2)}) copy-start(f32[64,512]{0,1:T(8,128)S(1)} %maximum_select_fusion) | copy-start | bytes 393220
  65.7 7.3 %collective-permute-start = (f32[64,512]{0,1:T(8,128)S(1)}, f32[64,512]{0,1:T(8,128)S(1)}, u32[]{:S(2)}, u32[]{:S(2)}) collective-permute-start(f32[64,512]{0,1:T(8,128)S(1)} %maximum_select_fusion), channel_id=1, source_target_pairs={{0,16},{1,17},{2,18},{3,19},{4,20},{5,21},{6,22},{7,23},{8,24},{9,... | collective-permute-start | bytes 393224 | tf_op jit(solution)/shard_map/ppermute | solution.py:12
  81.5 99.0 %all-gather.15.cloned.1.call-start = ((), (), s32[]{:S(2)}) async-start(), calls=%async_computation.2 | async-start | bytes 1179648 | tf_op jit(solution)/shard_map/all_gather | solution.py:68
  123.5 5.9 %copy-start.3 = (f32[64,512]{0,1:T(8,128)}, f32[64,512]{0,1:T(8,128)S(1)}, u32[]{:S(2)}) copy-start(f32[64,512]{0,1:T(8,128)S(1)} %maximum_select_fusion.2) | copy-start | bytes 393220
  123.5 7.3 %collective-permute-start.1 = (f32[64,512]{0,1:T(8,128)S(1)}, f32[64,512]{0,1:T(8,128)}, u32[]{:S(2)}, u32[]{:S(2)}) collective-permute-start(f32[64,512]{0,1:T(8,128)S(1)} %maximum_select_fusion.2), channel_id=1, source_target_pairs={{0,16},{1,17},{2,18},{3,19},{4,20},{5,21},{6,22},{7,23},{8,24},{9,... | collective-permute-start | bytes 393224 | tf_op jit(solution)/shard_map/ppermute | solution.py:12
  140.3 98.0 %all-gather.17.cloned.1.call-start = ((), (), s32[]{:S(2)}) async-start(), calls=%async_computation.3 | async-start | bytes 1179648 | tf_op jit(solution)/shard_map/all_gather | solution.py:68
  183.1 7.6 %collective-permute-start.2 = (f32[64,512]{0,1:T(8,128)}, f32[64,512]{0,1:T(8,128)S(1)}, u32[]{:S(2)}, u32[]{:S(2)}) collective-permute-start(f32[64,512]{0,1:T(8,128)} %maximum_select_fusion.4), channel_id=1, source_target_pairs={{0,16},{1,17},{2,18},{3,19},{4,20},{5,21},{6,22},{7,23},{8,24},{9,... | collective-permute-start | bytes 393224 | tf_op jit(solution)/shard_map/ppermute | solution.py:12
  198.2 96.8 %all-gather.19.cloned.1.call-start = ((), (), s32[]{:S(2)}) async-start(), calls=%async_computation.4 | async-start | bytes 1179648 | tf_op jit(solution)/shard_map/all_gather | solution.py:68
  240.1 7.3 %collective-permute-start.3 = (f32[64,512]{0,1:T(8,128)S(1)}, f32[64,512]{0,1:T(8,128)S(1)}, u32[]{:S(2)}, u32[]{:S(2)}) collective-permute-start(f32[64,512]{0,1:T(8,128)S(1)} %maximum_select_fusion.6), channel_id=1, source_target_pairs={{0,16},{1,17},{2,18},{3,19},{4,20},{5,21},{6,22},{7,23},{8,24},{9,... | collective-permute-start | bytes 393224 | tf_op jit(solution)/shard_map/ppermute | solution.py:12
Sparse Core Ops, SparseCore 0:
  20.9 42.9 all-gather.10
  81.6 39.9 all-gather.12
  140.4 40.0 all-gather.14
  198.3 39.8 all-gather.16
  255.0 39.9 all-gather.18
